TPU v7x, 512 devices: a whole 4x8x8 slice. The times are simulated.
512 devices in a mesh: seq: 128 (over z, y, core), dp: 4 (over x).
Axes of the slice: x: 4, y: 8, z: 8, core: 2. Of those that a mesh axis runs over, the one named last changes fastest.
Arguments:
- queries: bfloat16 [65536, 20, 128], P(('dp', 'seq')), parts along dimension 0, may hold values from -6 to 6
- keys: bfloat16 [65536, 20, 128], P(('dp', 'seq')), parts along dimension 0, may hold values from -4 to 4
- values: bfloat16 [65536, 20, 128], P(('dp', 'seq')), parts along dimension 0, may hold values from -6 to 6
- out_grad: bfloat16 [65536, 20, 128], P(('dp', 'seq')), parts along dimension 0, may hold values from -96 to 96
- block_mask: int32 [20, 128, 5], replicated, may hold values from 0 to 1, as said below
Outputs:
- query_grad: bfloat16 [65536, 20, 128], P(('dp', 'seq')), parts along dimension 0
- key_grad: bfloat16 [65536, 20, 128], P(('dp', 'seq')), parts along dimension 0
- value_grad: bfloat16 [65536, 20, 128], P(('dp', 'seq')), parts along dimension 0
There are 4 independent parts, one for each index of `dp`. A program takes and returns all parts, laid end to end along the dimension named above; an argument that names none is the same for every part. Nothing has to cross between parts.
Inputs may be any that keep to these rules, and one draw needn't show every extreme that they name: `block_mask`: entry j of row i names key block i + j - 2. The entry for j = 2 is always 1; entries naming blocks outside 0 to 127 are 0.
All inputs are finite; a program needn't handle non-finite values.
Results may differ from a plain program's by a relative error of at most 0.0075.
Values may be sent and summed in bfloat16 or wider, within the bound.
A program may use at most 64 MiB of HBM per device.

v0:
```python
import functools
import math

import jax
import jax.numpy as jnp
from jax import lax
from jax.experimental import pallas as pl
from jax.experimental.pallas import tpu as pltpu
from jax.sharding import PartitionSpec as P

NEG = -1e30
AHEAD = 2
LAG_TOTAL = 3
LAG_GRAD = 6
LAG_OUT = 9

NT = (((1,), (1,)), ((), ()))
NN = (((1,), (0,)), ((), ()))


def dot(a, b, dims):
    return lax.dot_general(a, b, dims, preferred_element_type=jnp.float32)


def kernel(
    seq_size,
    heads,
    scale,
    q_hbm,
    k_hbm,
    v_hbm,
    g_hbm,
    mask_hbm,
    dq_out,
    dk_out,
    dv_out,
    mask_ref,
    qg,
    kv,
    bias,
    exps,
    dps,
    w_ref,
    ds_ref,
    part,
    part_in,
    tot,
    tot_in,
    dq_own,
    dq_send,
    dq_in,
    obuf,
    recv_qg,
    recv_kv,
    recv_part,
    recv_tot,
    recv_dq,
    send_far,
    send_near,
    send_part,
    send_tot,
    send_dq,
    out_send,
    out_recv,
    mask_sem,
):
    nh = heads // 2
    me = lax.axis_index("seq")
    core = lax.rem(me, 2)
    other = 1 - core
    first = me - core
    left = first - 2
    right = first + 2
    has_left = first > 0
    has_right = right < seq_size
    sibling = first + other
    left_mate = left + core
    right_mate = right + core
    mine = pl.ds(pl.multiple_of(core * 128, 128), 128)
    theirs = pl.ds(pl.multiple_of(other * 128, 128), 128)

    barrier = pltpu.get_barrier_semaphore()

    def greet(to):
        pl.semaphore_signal(barrier, inc=1, device_id={"seq": to}, device_id_type=pl.DeviceIdType.MESH)

    greet(sibling)
    for side, base, present in ((0, left, has_left), (1, right, has_right)):

        @pl.when(present)
        def _():
            greet(base)
            greet(base + 1)

    mask_copy = pltpu.make_async_copy(mask_hbm, mask_ref, mask_sem)
    mask_copy.start()

    def remote(src, dst, send, recv, to):
        return pltpu.make_async_remote_copy(
            src_ref=src,
            dst_ref=dst,
            send_sem=send,
            recv_sem=recv,
            device_id={"seq": to},
            device_id_type=pl.DeviceIdType.MESH,
        )

    def wait_for(ref, sem):
        pltpu.make_async_copy(ref, ref, sem).wait()

    def span(s, c):
        return pl.ds(pl.multiple_of(s * 256 + c * 128, 128), 128)

    def to_mate(s, src, dst, send, recv, h):
        side = s // 2
        mate = right_mate if side else left_mate
        remote(src, dst.at[1 - side, h], send.at[side], recv.at[1 - side, h], mate).start()

    def load_own(h):
        src = core * nh + h
        pltpu.make_async_copy(q_hbm.at[src], qg.at[h, 0, span(1, core)], recv_qg.at[h, 1]).start()
        pltpu.make_async_copy(g_hbm.at[src], qg.at[h, 1, span(1, core)], recv_qg.at[h, 1]).start()
        pltpu.make_async_copy(k_hbm.at[src], kv.at[h, 0, mine], recv_kv.at[h]).start()
        pltpu.make_async_copy(v_hbm.at[src], kv.at[h, 1, mine], recv_kv.at[h]).start()

    def send_head(h):
        away = other * nh + h
        own_span = span(1, core)
        remote(q_hbm.at[away], qg.at[h, 0, own_span], send_near.at[0], recv_qg.at[h, 1], sibling).start()
        remote(g_hbm.at[away], qg.at[h, 1, own_span], send_near.at[1], recv_qg.at[h, 1], sibling).start()
        remote(k_hbm.at[away], kv.at[h, 0, mine], send_near.at[2], recv_kv.at[h], sibling).start()
        remote(v_hbm.at[away], kv.at[h, 1, mine], send_near.at[3], recv_kv.at[h], sibling).start()
        for side, base, present in ((0, left, has_left), (1, right, has_right)):
            slot = 2 - 2 * side

            @pl.when(present)
            def _():
                for half in range(2):
                    src = half * nh + h
                    to = base + half
                    remote(
                        q_hbm.at[src], qg.at[h, 0, span(slot, core)], send_far.at[side, 0], recv_qg.at[h, slot], to
                    ).start()
                    remote(
                        g_hbm.at[src], qg.at[h, 1, span(slot, core)], send_far.at[side, 1], recv_qg.at[h, slot], to
                    ).start()

    pl.semaphore_wait(barrier, 1 + 2 * has_left.astype(jnp.int32) + 2 * has_right.astype(jnp.int32))

    for h in range(AHEAD):
        send_head(h)
    for h in range(nh):
        load_own(h)

    mask_copy.wait()
    planes = mask_ref[...]
    block_at = lax.broadcasted_iota(jnp.int32, planes.shape, 2)
    for t in range(6):
        picked = jnp.where(block_at == first - 2 + t, planes, 0)
        allowed = jnp.max(picked, axis=2, keepdims=True)
        bias[t] = jnp.broadcast_to(jnp.where(allowed > 0, 0.0, NEG), bias.shape[1:])
    for side, present in ((0, has_left), (1, has_right)):

        @pl.when(jnp.logical_not(present))
        def _():
            edge = slice(512 * side, 512 * side + 256)
            qg[:, :, edge, :] = jnp.zeros((nh, 2, 256, 128), jnp.bfloat16)
            part_in[side, :, 0:2, :] = jnp.full((nh, 2, 128), NEG, jnp.float32)
            part_in[side, :, 2:8, :] = jnp.zeros((nh, 6, 128), jnp.float32)
            tot_in[side] = jnp.zeros(tot_in.shape[1:], jnp.float32)
            dq_in[side] = jnp.zeros(dq_in.shape[1:], jnp.bfloat16)

    zero = jnp.zeros((128, 128), jnp.bfloat16)
    for ref in (w_ref, ds_ref):
        ref[128:256, 0:128] = zero
        ref[0:128, 640:768] = zero
    part[...] = jnp.zeros(part.shape, jnp.float32)
    tot[...] = jnp.zeros(tot.shape, jnp.float32)

    log_scale = scale * math.log2(math.e)

    def on_side(s, act):
        if s == 1:
            act()
        else:
            pl.when(has_left if s == 0 else has_right)(act)

    def key_blocks(t):
        return (0,) if t == 0 else (1,) if t == 5 else (0, 1)

    def scores(h):
        wait_for(kv.at[h], recv_kv.at[h])
        keys = kv[h, 0]
        values = kv[h, 1]
        for s in (1, 0, 2):
            on_side(s, lambda: wait_for(qg.at[h, :, s * 256 : s * 256 + 256], recv_qg.at[h, s]))
            raw = dot(keys, qg[h, 0, s * 256 : s * 256 + 256], NT)
            dp = dot(values, qg[h, 1, s * 256 : s * 256 + 256], NT)
            for a in range(2):
                t = 2 * s + a
                cols = slice(a * 128, a * 128 + 128)
                put = slice(t * 128, t * 128 + 128)
                logits = {}
                for b in key_blocks(t):
                    row = bias[t, b + 4 - t, pl.ds(core * nh + h, 1), :]
                    logits[b] = raw[b * 128 : b * 128 + 128, cols] * log_scale + row
                peak = functools.reduce(
                    jnp.maximum, [jnp.max(x, axis=0, keepdims=True) for x in logits.values()]
                )
                total = 0.0
                delta = 0.0
                for b, x in logits.items():
                    rows = slice(b * 128, b * 128 + 128)
                    e = jnp.exp2(x - peak)
                    g = dp[rows, cols]
                    exps[h, rows, put] = e
                    dps[h, rows, put] = g
                    total = total + jnp.sum(e, axis=0, keepdims=True)
                    delta = delta + jnp.sum(e * g, axis=0, keepdims=True)
                part[s, h, a : a + 1, :] = peak
                part[s, h, 2 + a : 3 + a, :] = total
                part[s, h, 4 + a : 5 + a, :] = delta
            if s != 1:
                on_side(s, lambda: to_mate(s, part.at[s, h], part_in, send_part, recv_part, h))

    def totals(h):
        for s in (0, 2):
            on_side(s, lambda: wait_for(part_in.at[s // 2, h], recv_part.at[s // 2, h]))
        tiles = [part[1, h], part_in[0, h], part_in[1, h]]
        peak = functools.reduce(jnp.maximum, [x[0:2] for x in tiles])
        total = 0.0
        delta = 0.0
        for x in tiles:
            f = jnp.exp2(x[0:2] - peak)
            total = total + x[2:4] * f
            delta = delta + x[4:6] * f
        inverse = 1.0 / total
        tot[h, 0:2, :] = peak
        tot[h, 2:4, :] = inverse
        tot[h, 4:6, :] = delta * inverse
        for s in (0, 2):
            on_side(s, lambda: to_mate(s, tot.at[h], tot_in, send_tot, recv_tot, h))

    def give(h, which, out, value):
        value = value.astype(jnp.bfloat16)
        obuf[which, h] = value
        out[core * nh + h] = obuf[which, h, mine]
        remote(
            obuf.at[which, h, theirs], out.at[core * nh + h], out_send.at[which], out_recv.at[which], sibling
        ).start()

    def grads(h):
        for s in (0, 2):
            on_side(s, lambda: wait_for(tot_in.at[s // 2, h], recv_tot.at[s // 2, h]))
        tiles = [tot_in[0, h], tot[h], tot_in[1, h]]
        for t in range(6):
            s, a = divmod(t, 2)
            put = slice(t * 128, t * 128 + 128)
            tile = tiles[s]
            f = jnp.exp2(part[s, h, a : a + 1, :] - tile[a : a + 1]) * tile[2 + a : 3 + a]
            shift = tile[4 + a : 5 + a]
            for b in key_blocks(t):
                rows = slice(b * 128, b * 128 + 128)
                w = exps[h, rows, put] * f
                w_ref[rows, put] = w.astype(jnp.bfloat16)
                ds_ref[rows, put] = (w * (dps[h, rows, put] - shift)).astype(jnp.bfloat16)
        ds = ds_ref[...]
        dq = dot(kv[h, 0].T, ds, NN)
        for s in (0, 2):
            dq_send[s // 2, h] = dq[:, s * 256 : s * 256 + 256].astype(jnp.bfloat16)
            on_side(s, lambda: to_mate(s, dq_send.at[s // 2, h], dq_in, send_dq, recv_dq, h))
        dq_own[h] = dq[:, 256:512]
        give(h, 1, dk_out, dot(ds, qg[h, 0], NN) * scale)
        give(h, 2, dv_out, dot(w_ref[...], qg[h, 1], NN))

    def outputs(h):
        for s in (0, 2):
            on_side(s, lambda: wait_for(dq_in.at[s // 2, h], recv_dq.at[s // 2, h]))
        dq = dq_own[h] + dq_in[0, h].astype(jnp.float32) + dq_in[1, h].astype(jnp.float32)
        give(h, 0, dq_out, (dq * scale).T)

    def step(i, carry):
        @pl.when(i + AHEAD < nh)
        def _():
            send_head(i + AHEAD)

        @pl.when((i >= LAG_TOTAL) & (i < nh + LAG_TOTAL))
        def _():
            totals(i - LAG_TOTAL)

        @pl.when((i >= LAG_GRAD) & (i < nh + LAG_GRAD))
        def _():
            grads(i - LAG_GRAD)

        @pl.when(i >= LAG_OUT)
        def _():
            outputs(i - LAG_OUT)

        @pl.when(i < nh)
        def _():
            scores(i)

        return carry

    lax.fori_loop(0, nh + LAG_OUT, step, 0)

    for side, present in ((0, has_left), (1, has_right)):

        @pl.when(present)
        def _():
            wait_for(q_hbm, send_far.at[side, 0])
            wait_for(g_hbm, send_far.at[side, 1])
            wait_for(part.at[0], send_part.at[side])
            wait_for(tot, send_tot.at[side])
            wait_for(dq_send.at[side], send_dq.at[side])

    for which, ref in enumerate((q_hbm, g_hbm, k_hbm, v_hbm)):
        wait_for(ref.at[0:nh], send_near.at[which])
    for which, ref in enumerate((dq_out, dk_out, dv_out)):
        half = ref.at[0:nh]
        wait_for(half, out_send.at[which])
        wait_for(half, out_recv.at[which])


def store(dq_ref, dk_ref, dv_ref, dq_hbm, dk_hbm, dv_hbm, sem):
    copies = [
        pltpu.make_async_copy(src, dst, sem.at[i])
        for i, (src, dst) in enumerate(((dq_ref, dq_hbm), (dk_ref, dk_hbm), (dv_ref, dv_hbm)))
    ]
    for copy in copies:
        copy.start()
    for copy in copies:
        copy.wait()


def per_device(queries, keys, values, out_grad, block_mask, seq_size):
    tokens, heads, width = queries.shape
    nh = heads // 2
    args = [jnp.transpose(x, (1, 0, 2)) for x in (queries, keys, values, out_grad)]
    mask = jnp.transpose(block_mask, (2, 0, 1))
    out = jax.ShapeDtypeStruct((heads, tokens, width), jnp.bfloat16)
    bf16, f32 = jnp.bfloat16, jnp.float32
    dma = pltpu.SemaphoreType.DMA
    hbm_spec = pl.BlockSpec(memory_space=pltpu.HBM)
    vmem_spec = pl.BlockSpec(memory_space=pltpu.VMEM)
    result = pl.pallas_call(
        functools.partial(kernel, seq_size, heads, 1.0 / math.sqrt(width)),
        out_shape=(out, out, out),
        in_specs=[hbm_spec] * 5,
        out_specs=(vmem_spec,) * 3,
        scratch_shapes=[
            pltpu.VMEM(mask.shape, jnp.int32),
            pltpu.VMEM((nh, 2, 768, 128), bf16),
            pltpu.VMEM((nh, 2, 256, 128), bf16),
            pltpu.VMEM((6, 5, heads, 128), f32),
            pltpu.VMEM((nh, 256, 768), f32),
            pltpu.VMEM((nh, 256, 768), f32),
            pltpu.VMEM((256, 768), bf16),
            pltpu.VMEM((256, 768), bf16),
            pltpu.VMEM((3, nh, 8, 128), f32),
            pltpu.VMEM((2, nh, 8, 128), f32),
            pltpu.VMEM((nh, 8, 128), f32),
            pltpu.VMEM((2, nh, 8, 128), f32),
            pltpu.VMEM((nh, 128, 256), f32),
            pltpu.VMEM((2, nh, 128, 256), bf16),
            pltpu.VMEM((2, nh, 128, 256), bf16),
            pltpu.VMEM((3, nh, 256, 128), bf16),
            dma((nh, 3)),
            dma((nh,)),
            dma((2, nh)),
            dma((2, nh)),
            dma((2, nh)),
            dma((2, 2)),
            dma((4,)),
            dma((2,)),
            dma((2,)),
            dma((2,)),
            dma((3,)),
            dma((3,)),
            dma,
        ],
        compiler_params=pltpu.CompilerParams(
            collective_id=0, has_side_effects=True, vmem_limit_bytes=53000 * 1024
        ),
        name="block_attention",
    )(*args, mask)
    result = pl.pallas_call(
        store,
        out_shape=(out, out, out),
        in_specs=[vmem_spec] * 3,
        out_specs=(hbm_spec,) * 3,
        scratch_shapes=[dma((3,))],
        compiler_params=pltpu.CompilerParams(vmem_limit_bytes=4 * 1024 * 1024),
        name="store_gradients",
    )(*result)
    return tuple(jnp.transpose(x, (1, 0, 2)) for x in result)


def solution(mesh):
    spec = P(("dp", "seq"), None, None)
    return jax.shard_map(
        functools.partial(per_device, seq_size=mesh.shape["seq"]),
        mesh=mesh,
        in_specs=(spec, spec, spec, spec, P()),
        out_specs=(spec, spec, spec),
        check_vma=False,
    )
```

profile of v0, /device:TPU:1, one launch (start us, length us, event | category | flops | bytes accessed | tf_op | source)
XLA Modules:
  0.0 59.3 jit_solution(18085262942376055734)
XLA Ops:
  0.6 0.0 copy-start
  0.6 0.8 %copy-done = s32[20,128,5]{1,0,2:T(8,128)S(1)} copy-done((s32[20,128,5]{1,0,2:T(8,128)S(1)}, s32[20,128,5]{1,0,2:T(8,128)}, u32[]{:S(2)}) %copy-start) | copy-done | bytes 51224
  1.5 56.6 %block_attention.1 = (bf16[20,128,128]{2,1,0:T(8,128)(2,1)S(1)}, bf16[20,128,128]{2,1,0:T(8,128)(2,1)S(1)}, bf16[20,128,128]{2,1,0:T(8,128)(2,1)S(1)}) custom-call(bf16[20,128,128]{2,1,0:T(8,128)(2,1)} %bitcast.9, bf16[20,128,128]{2,1,0:T(8,128)(2,1)} %bitcast.10, bf16[20,128,128]{2,1,0:T(8,128)(2,1)} %bitcast.11, bf16[20,128,128]{2,1,0:T(8,128)(2,1)} %bitcast.12, ...), custom_call_target="tpu_custom_call" | custom-call | tf_op jit(solution)/shard_map/block_attention/pallas_call | solution.py:346
  58.0 1.3 %store_gradients.1 = (bf16[20,128,128]{2,1,0:T(8,128)(2,1)}, bf16[20,128,128]{2,1,0:T(8,128)(2,1)}, bf16[20,128,128]{2,1,0:T(8,128)(2,1)}) custom-call(bf16[20,128,128]{2,1,0:T(8,128)(2,1)S(1)} %get-tuple-element.9.dq_ref, bf16[20,128,128]{2,1,0:T(8,128)(2,1)S(1)} %get-tuple-element.10.dk_ref, bf16[20,128,128]{2,1,0:T(8,128)(2,1)S(1)} %get-tuple-element.11.dv_ref), custom_call_target="tpu_custom_call" | custom-call | tf_op jit(solution)/shard_map/store_gradients/pallas_call | solution.py:387
Async XLA Ops:
  0.6 0.8 %copy-start = (s32[20,128,5]{1,0,2:T(8,128)S(1)}, s32[20,128,5]{1,0,2:T(8,128)}, u32[]{:S(2)}) copy-start(s32[20,128,5]{1,0,2:T(8,128)} %param.9) | copy-start | bytes 153604
where the time goes:
time: 59.5 us; the launch traced here: 59.3 us
  Pallas kernels  57.9 us (97%)
  local copies, waits for them, and re-layouts  0.82 us (1%)
  between operations  0.65 us (1%)
    pallas_call x1, Pallas kernels, per_device(): pl.pallas_call(functools.partial(kernel, seq_size, heads, 1.0 / math.sqrt...  56.6 us
    pallas_call x1, Pallas kernels, per_device(): pl.pallas_call(store, out_shape=(out, out, out), in_specs=[vmem_spec] * 3...  1.3 us

commit v1 on v0

--- a/solution.py
+++ b/solution.py
@@ -42,11 +42,13 @@
     dps,
     w_ref,
     ds_ref,
+    peaks,
     part,
     part_in,
     tot,
     tot_in,
     dq_own,
+    dq_pass,
     dq_send,
     dq_in,
     obuf,
@@ -55,11 +57,13 @@
     recv_part,
     recv_tot,
     recv_dq,
+    recv_pass,
     send_far,
     send_near,
     send_part,
     send_tot,
     send_dq,
+    send_pass,
     out_send,
     out_recv,
     mask_sem,
@@ -145,12 +149,17 @@
                         g_hbm.at[src], qg.at[h, 1, span(slot, core)], send_far.at[side, 1], recv_qg.at[h, slot], to
                     ).start()
 
+    for h in range(nh):
+        load_own(h)
+    zero = jnp.zeros((128, 128), jnp.bfloat16)
+    for ref in (w_ref, ds_ref):
+        ref[128:256, 0:128] = zero
+        ref[0:128, 640:768] = zero
+
     pl.semaphore_wait(barrier, 1 + 2 * has_left.astype(jnp.int32) + 2 * has_right.astype(jnp.int32))
 
     for h in range(AHEAD):
         send_head(h)
-    for h in range(nh):
-        load_own(h)
 
     mask_copy.wait()
     planes = mask_ref[...]
@@ -166,16 +175,9 @@
             edge = slice(512 * side, 512 * side + 256)
             qg[:, :, edge, :] = jnp.zeros((nh, 2, 256, 128), jnp.bfloat16)
             part_in[side, :, 0:2, :] = jnp.full((nh, 2, 128), NEG, jnp.float32)
-            part_in[side, :, 2:8, :] = jnp.zeros((nh, 6, 128), jnp.float32)
+            part_in[side, :, 2:4, :] = jnp.zeros((nh, 2, 128), jnp.float32)
             tot_in[side] = jnp.zeros(tot_in.shape[1:], jnp.float32)
             dq_in[side] = jnp.zeros(dq_in.shape[1:], jnp.bfloat16)
-
-    zero = jnp.zeros((128, 128), jnp.bfloat16)
-    for ref in (w_ref, ds_ref):
-        ref[128:256, 0:128] = zero
-        ref[0:128, 640:768] = zero
-    part[...] = jnp.zeros(part.shape, jnp.float32)
-    tot[...] = jnp.zeros(tot.shape, jnp.float32)
 
     log_scale = scale * math.log2(math.e)
 
@@ -217,9 +219,9 @@
                     dps[h, rows, put] = g
                     total = total + jnp.sum(e, axis=0, keepdims=True)
                     delta = delta + jnp.sum(e * g, axis=0, keepdims=True)
-                part[s, h, a : a + 1, :] = peak
-                part[s, h, 2 + a : 3 + a, :] = total
-                part[s, h, 4 + a : 5 + a, :] = delta
+                peaks[s, h, a : a + 1, :] = peak
+                part[s, h, a : a + 1, :] = peak + jnp.log2(total)
+                part[s, h, 2 + a : 3 + a, :] = delta / total
             if s != 1:
                 on_side(s, lambda: to_mate(s, part.at[s, h], part_in, send_part, recv_part, h))
 
@@ -232,12 +234,10 @@
         delta = 0.0
         for x in tiles:
             f = jnp.exp2(x[0:2] - peak)
-            total = total + x[2:4] * f
-            delta = delta + x[4:6] * f
-        inverse = 1.0 / total
-        tot[h, 0:2, :] = peak
-        tot[h, 2:4, :] = inverse
-        tot[h, 4:6, :] = delta * inverse
+            total = total + f
+            delta = delta + x[2:4] * f
+        tot[h, 0:2, :] = peak + jnp.log2(total)
+        tot[h, 2:4, :] = delta / total
         for s in (0, 2):
             on_side(s, lambda: to_mate(s, tot.at[h], tot_in, send_tot, recv_tot, h))
 
@@ -257,8 +257,8 @@
             s, a = divmod(t, 2)
             put = slice(t * 128, t * 128 + 128)
             tile = tiles[s]
-            f = jnp.exp2(part[s, h, a : a + 1, :] - tile[a : a + 1]) * tile[2 + a : 3 + a]
-            shift = tile[4 + a : 5 + a]
+            f = jnp.exp2(peaks[s, h, a : a + 1, :] - tile[a : a + 1])
+            shift = tile[2 + a : 3 + a]
             for b in key_blocks(t):
                 rows = slice(b * 128, b * 128 + 128)
                 w = exps[h, rows, put] * f
@@ -266,18 +266,36 @@
                 ds_ref[rows, put] = (w * (dps[h, rows, put] - shift)).astype(jnp.bfloat16)
         ds = ds_ref[...]
         dq = dot(kv[h, 0].T, ds, NN)
-        for s in (0, 2):
-            dq_send[s // 2, h] = dq[:, s * 256 : s * 256 + 256].astype(jnp.bfloat16)
-            on_side(s, lambda: to_mate(s, dq_send.at[s // 2, h], dq_in, send_dq, recv_dq, h))
-        dq_own[h] = dq[:, 256:512]
-        give(h, 1, dk_out, dot(ds, qg[h, 0], NN) * scale)
-        give(h, 2, dv_out, dot(w_ref[...], qg[h, 1], NN))
+        head = core * nh + h
+        for side, base, present in ((0, left, has_left), (1, right, has_right)):
+            for a in range(2):
+                t = 4 * side + a
+                dq_send[side, h, a] = dq[:, t * 128 : t * 128 + 128].astype(jnp.bfloat16)
+
+            @pl.when(present)
+            def _():
+                for a in range(2):
+                    remote(
+                        dq_send.at[side, h, a],
+                        dq_in.at[1 - side, head],
+                        send_dq.at[side],
+                        recv_dq.at[1 - side, head],
+                        base + a,
+                    ).start()
+
+        dq_own[head] = jnp.where(core == 0, dq[:, 256:384], dq[:, 384:512])
+        dq_pass[h] = jnp.where(core == 0, dq[:, 384:512], dq[:, 256:384])
+        remote(dq_pass.at[h], dq_own.at[head], send_pass, recv_pass.at[h], sibling).start()
+        give(h, 0, dk_out, dot(ds, qg[h, 0], NN) * scale)
+        give(h, 1, dv_out, dot(w_ref[...], qg[h, 1], NN))
 
     def outputs(h):
-        for s in (0, 2):
-            on_side(s, lambda: wait_for(dq_in.at[s // 2, h], recv_dq.at[s // 2, h]))
-        dq = dq_own[h] + dq_in[0, h].astype(jnp.float32) + dq_in[1, h].astype(jnp.float32)
-        give(h, 0, dq_out, (dq * scale).T)
+        wait_for(dq_own.at[other * nh + h], recv_pass.at[h])
+        for g in (h, nh + h):
+            for s in (0, 2):
+                on_side(s, lambda: wait_for(dq_in.at[s // 2, g], recv_dq.at[s // 2, g]))
+            dq = dq_own[g] + dq_in[0, g].astype(jnp.float32) + dq_in[1, g].astype(jnp.float32)
+            dq_out[g] = (dq * scale).T.astype(jnp.bfloat16)
 
     def step(i, carry):
         @pl.when(i + AHEAD < nh)
@@ -316,7 +334,8 @@
 
     for which, ref in enumerate((q_hbm, g_hbm, k_hbm, v_hbm)):
         wait_for(ref.at[0:nh], send_near.at[which])
-    for which, ref in enumerate((dq_out, dk_out, dv_out)):
+    wait_for(dq_pass, send_pass)
+    for which, ref in enumerate((dk_out, dv_out)):
         half = ref.at[0:nh]
         wait_for(half, out_send.at[which])
         wait_for(half, out_recv.at[which])
@@ -333,11 +352,15 @@
         copy.wait()
 
 
+def in_hbm(x):
+    return pltpu.with_memory_space_constraint(x, pltpu.HBM)
+
+
 def per_device(queries, keys, values, out_grad, block_mask, seq_size):
     tokens, heads, width = queries.shape
     nh = heads // 2
-    args = [jnp.transpose(x, (1, 0, 2)) for x in (queries, keys, values, out_grad)]
-    mask = jnp.transpose(block_mask, (2, 0, 1))
+    args = [in_hbm(jnp.transpose(x, (1, 0, 2))) for x in (queries, keys, values, out_grad)]
+    mask = in_hbm(jnp.transpose(block_mask, (2, 0, 1)))
     out = jax.ShapeDtypeStruct((heads, tokens, width), jnp.bfloat16)
     bf16, f32 = jnp.bfloat16, jnp.float32
     dma = pltpu.SemaphoreType.DMA
@@ -357,30 +380,34 @@
             pltpu.VMEM((nh, 256, 768), f32),
             pltpu.VMEM((256, 768), bf16),
             pltpu.VMEM((256, 768), bf16),
-            pltpu.VMEM((3, nh, 8, 128), f32),
-            pltpu.VMEM((2, nh, 8, 128), f32),
-            pltpu.VMEM((nh, 8, 128), f32),
-            pltpu.VMEM((2, nh, 8, 128), f32),
-            pltpu.VMEM((nh, 128, 256), f32),
-            pltpu.VMEM((2, nh, 128, 256), bf16),
-            pltpu.VMEM((2, nh, 128, 256), bf16),
-            pltpu.VMEM((3, nh, 256, 128), bf16),
+            pltpu.VMEM((3, nh, 2, 128), f32),
+            pltpu.VMEM((3, nh, 4, 128), f32),
+            pltpu.VMEM((2, nh, 4, 128), f32),
+            pltpu.VMEM((nh, 4, 128), f32),
+            pltpu.VMEM((2, nh, 4, 128), f32),
+            pltpu.VMEM((heads, 128, 128), f32),
+            pltpu.VMEM((nh, 128, 128), f32),
+            pltpu.VMEM((2, nh, 2, 128, 128), bf16),
+            pltpu.VMEM((2, heads, 128, 128), bf16),
+            pltpu.VMEM((2, nh, 256, 128), bf16),
             dma((nh, 3)),
             dma((nh,)),
             dma((2, nh)),
             dma((2, nh)),
-            dma((2, nh)),
+            dma((2, heads)),
+            dma((nh,)),
             dma((2, 2)),
             dma((4,)),
             dma((2,)),
             dma((2,)),
             dma((2,)),
-            dma((3,)),
-            dma((3,)),
+            dma,
+            dma((2,)),
+            dma((2,)),
             dma,
         ],
         compiler_params=pltpu.CompilerParams(
-            collective_id=0, has_side_effects=True, vmem_limit_bytes=53000 * 1024
+            collective_id=0, has_side_effects=True, vmem_limit_bytes=48000 * 1024
         ),
         name="block_attention",
     )(*args, mask)

time: 59.5 us -> 56.8 us (0.955)
  Pallas kernels: 57.9 us -> 56 us
  local copies, waits for them, and re-layouts: 0.82 us -> 0 us
    pallas_call x1, Pallas kernels: 56.6 us -> 54.7 us  [per_device(): pl.pallas_call(functools.partial(kernel, seq_size, heads, 1.0 / math.sqrt...]
    unnamed x2 -> x0, local copies, waits for them, and re-layouts: 0.82 us -> none
where the time goes in v1:
time: 56.8 us; the launch traced here: 56.6 us
  Pallas kernels  56 us (99%)
  between operations  0.64 us (1%)
    pallas_call x1, Pallas kernels, per_device(): pl.pallas_call(functools.partial(kernel, seq_size, heads, 1.0 / math.sqrt...  54.7 us
    pallas_call x1, Pallas kernels, per_device(): pl.pallas_call(store, out_shape=(out, out, out), in_specs=[vmem_spec] * 3...  1.3 us

profile of v1, /device:TPU:1, one launch (start us, length us, event | category | flops | bytes accessed | tf_op | source)
XLA Modules:
  0.0 56.6 jit_solution(14639886899669246136)
XLA Ops:
  0.6 54.7 %block_attention.1 = (bf16[20,128,128]{2,1,0:T(8,128)(2,1)S(1)}, bf16[20,128,128]{2,1,0:T(8,128)(2,1)S(1)}, bf16[20,128,128]{2,1,0:T(8,128)(2,1)S(1)}) custom-call(bf16[20,128,128]{2,1,0:T(8,128)(2,1)} %bitcast.8, bf16[20,128,128]{2,1,0:T(8,128)(2,1)} %bitcast.9, bf16[20,128,128]{2,1,0:T(8,128)(2,1)} %bitcast.10, bf16[20,128,128]{2,1,0:T(8,128)(2,1)} %bitcast.11, ...), custom_call_target="tpu_custom_call" | custom-call | tf_op jit(solution)/shard_map/block_attention/pallas_call | solution.py:369
  55.3 1.3 %store_gradients.1 = (bf16[20,128,128]{2,1,0:T(8,128)(2,1)}, bf16[20,128,128]{2,1,0:T(8,128)(2,1)}, bf16[20,128,128]{2,1,0:T(8,128)(2,1)}) custom-call(bf16[20,128,128]{2,1,0:T(8,128)(2,1)S(1)} %get-tuple-element.9.dq_ref, bf16[20,128,128]{2,1,0:T(8,128)(2,1)S(1)} %get-tuple-element.10.dk_ref, bf16[20,128,128]{2,1,0:T(8,128)(2,1)S(1)} %get-tuple-element.11.dv_ref), custom_call_target="tpu_custom_call" | custom-call | tf_op jit(solution)/shard_map/store_gradients/pallas_call | solution.py:414

commit v2 on v1

--- a/solution.py
+++ b/solution.py
@@ -10,9 +10,9 @@
 
 NEG = -1e30
 AHEAD = 2
-LAG_TOTAL = 3
-LAG_GRAD = 6
-LAG_OUT = 9
+LAG_TOTAL = 4
+LAG_GRAD = 7
+LAG_OUT = 11
 
 NT = (((1,), (1,)), ((), ()))
 NN = (((1,), (0,)), ((), ()))
@@ -67,6 +67,7 @@
     out_send,
     out_recv,
     mask_sem,
+    entered,
 ):
     nh = heads // 2
     me = lax.axis_index("seq")
@@ -85,16 +86,22 @@
 
     barrier = pltpu.get_barrier_semaphore()
 
-    def greet(to):
-        pl.semaphore_signal(barrier, inc=1, device_id={"seq": to}, device_id_type=pl.DeviceIdType.MESH)
-
-    greet(sibling)
-    for side, base, present in ((0, left, has_left), (1, right, has_right)):
-
-        @pl.when(present)
-        def _():
-            greet(base)
-            greet(base + 1)
+    def greet(sem, to):
+        pl.semaphore_signal(sem, inc=1, device_id={"seq": to}, device_id_type=pl.DeviceIdType.MESH)
+
+    part_zero = lax.axis_index("dp") == 0
+    enters_last = part_zero & (me == 0)
+    meets_last = part_zero & (me > 0) & (me < 4)
+
+    @pl.when(jnp.logical_not(enters_last))
+    def _():
+        greet(barrier, sibling)
+        for base, present in ((left, has_left), (right, has_right)):
+
+            @pl.when(present)
+            def _():
+                greet(barrier, base)
+                greet(barrier, base + 1)
 
     mask_copy = pltpu.make_async_copy(mask_hbm, mask_ref, mask_sem)
     mask_copy.start()
@@ -127,27 +134,44 @@
         pltpu.make_async_copy(k_hbm.at[src], kv.at[h, 0, mine], recv_kv.at[h]).start()
         pltpu.make_async_copy(v_hbm.at[src], kv.at[h, 1, mine], recv_kv.at[h]).start()
 
-    def send_head(h):
+    def send_near_head(h):
         away = other * nh + h
         own_span = span(1, core)
         remote(q_hbm.at[away], qg.at[h, 0, own_span], send_near.at[0], recv_qg.at[h, 1], sibling).start()
         remote(g_hbm.at[away], qg.at[h, 1, own_span], send_near.at[1], recv_qg.at[h, 1], sibling).start()
         remote(k_hbm.at[away], kv.at[h, 0, mine], send_near.at[2], recv_kv.at[h], sibling).start()
         remote(v_hbm.at[away], kv.at[h, 1, mine], send_near.at[3], recv_kv.at[h], sibling).start()
-        for side, base, present in ((0, left, has_left), (1, right, has_right)):
-            slot = 2 - 2 * side
+
+    def send_far_head(h, side, half):
+        src = half * nh + h
+        slot = 2 - 2 * side
+        to = (right if side else left) + half
+        place = span(slot, core)
+        remote(q_hbm.at[src], qg.at[h, 0, place], send_far.at[side, 0], recv_qg.at[h, slot], to).start()
+        remote(g_hbm.at[src], qg.at[h, 1, place], send_far.at[side, 1], recv_qg.at[h, slot], to).start()
+
+    def send_head(h):
+        send_near_head(h)
+        for side, present in ((0, has_left), (1, has_right)):
 
             @pl.when(present)
             def _():
                 for half in range(2):
-                    src = half * nh + h
-                    to = base + half
-                    remote(
-                        q_hbm.at[src], qg.at[h, 0, span(slot, core)], send_far.at[side, 0], recv_qg.at[h, slot], to
-                    ).start()
-                    remote(
-                        g_hbm.at[src], qg.at[h, 1, span(slot, core)], send_far.at[side, 1], recv_qg.at[h, slot], to
-                    ).start()
+                    send_far_head(h, side, half)
+
+    def send_head_early(h):
+        pl.when(jnp.logical_not(meets_last & (me == 1)))(lambda: send_near_head(h))
+        pl.when(has_left & jnp.logical_not(meets_last))(lambda: send_far_head(h, 0, 0))
+        pl.when(has_left)(lambda: send_far_head(h, 0, 1))
+
+        @pl.when(has_right)
+        def _():
+            for half in range(2):
+                send_far_head(h, 1, half)
+
+    def send_head_late(h):
+        pl.when(me == 1)(lambda: send_near_head(h))
+        pl.when(me > 1)(lambda: send_far_head(h, 0, 0))
 
     for h in range(nh):
         load_own(h)
@@ -156,10 +180,23 @@
         ref[128:256, 0:128] = zero
         ref[0:128, 640:768] = zero
 
-    pl.semaphore_wait(barrier, 1 + 2 * has_left.astype(jnp.int32) + 2 * has_right.astype(jnp.int32))
+    early = 1 + 2 * has_left.astype(jnp.int32) + 2 * has_right.astype(jnp.int32) - meets_last.astype(jnp.int32)
+    pl.semaphore_wait(barrier, early)
+
+    @pl.when(enters_last)
+    def _():
+        for to in (sibling, right, right + 1):
+            greet(entered, to)
+
 
     for h in range(AHEAD):
-        send_head(h)
+        send_head_early(h)
+
+    @pl.when(meets_last)
+    def _():
+        pl.semaphore_wait(entered, 1)
+        for h in range(AHEAD):
+            send_head_late(h)
 
     mask_copy.wait()
     planes = mask_ref[...]
@@ -405,6 +442,7 @@
             dma((2,)),
             dma((2,)),
             dma,
+            pltpu.SemaphoreType.REGULAR,
         ],
         compiler_params=pltpu.CompilerParams(
             collective_id=0, has_side_effects=True, vmem_limit_bytes=48000 * 1024

time: 56.8 us -> 54.5 us (0.960)
  Pallas kernels: 56 us -> 53.4 us
    pallas_call x1, Pallas kernels: 54.7 us -> 52.1 us  [per_device(): pl.pallas_call(functools.partial(kernel, seq_size, heads, 1.0 / math.sqrt...]
where the time goes in v2:
time: 54.5 us; the launch traced here: 54.1 us
  Pallas kernels  53.4 us (98%)
  between operations  0.64 us (1%)
    pallas_call x1, Pallas kernels, per_device(): pl.pallas_call(functools.partial(kernel, seq_size, heads, 1.0 / math.sqrt...  52.1 us
    pallas_call x1, Pallas kernels, per_device(): pl.pallas_call(store, out_shape=(out, out, out), in_specs=[vmem_spec] * 3...  1.3 us

profile of v2, /device:TPU:1, one launch (start us, length us, event | category | flops | bytes accessed | tf_op | source)
XLA Modules:
  0.0 54.1 jit_solution(7551296613733887266)
XLA Ops:
  0.6 52.1 %block_attention.1 = (bf16[20,128,128]{2,1,0:T(8,128)(2,1)S(1)}, bf16[20,128,128]{2,1,0:T(8,128)(2,1)S(1)}, bf16[20,128,128]{2,1,0:T(8,128)(2,1)S(1)}) custom-call(bf16[20,128,128]{2,1,0:T(8,128)(2,1)} %bitcast.8, bf16[20,128,128]{2,1,0:T(8,128)(2,1)} %bitcast.9, bf16[20,128,128]{2,1,0:T(8,128)(2,1)} %bitcast.10, bf16[20,128,128]{2,1,0:T(8,128)(2,1)} %bitcast.11, ...), custom_call_target="tpu_custom_call" | custom-call | tf_op jit(solution)/shard_map/block_attention/pallas_call | solution.py:406
  52.8 1.3 %store_gradients.1 = (bf16[20,128,128]{2,1,0:T(8,128)(2,1)}, bf16[20,128,128]{2,1,0:T(8,128)(2,1)}, bf16[20,128,128]{2,1,0:T(8,128)(2,1)}) custom-call(bf16[20,128,128]{2,1,0:T(8,128)(2,1)S(1)} %get-tuple-element.9.dq_ref, bf16[20,128,128]{2,1,0:T(8,128)(2,1)S(1)} %get-tuple-element.10.dk_ref, bf16[20,128,128]{2,1,0:T(8,128)(2,1)S(1)} %get-tuple-element.11.dv_ref), custom_call_target="tpu_custom_call" | custom-call | tf_op jit(solution)/shard_map/store_gradients/pallas_call | solution.py:452

commit v3 on v2

--- a/solution.py
+++ b/solution.py
@@ -151,13 +151,14 @@
         remote(g_hbm.at[src], qg.at[h, 1, place], send_far.at[side, 1], recv_qg.at[h, slot], to).start()
 
     def send_head(h):
-        send_near_head(h)
         for side, present in ((0, has_left), (1, has_right)):
 
             @pl.when(present)
             def _():
                 for half in range(2):
                     send_far_head(h, side, half)
+
+        send_near_head(h)
 
     def send_head_early(h):
         pl.when(jnp.logical_not(meets_last & (me == 1)))(lambda: send_near_head(h))
@@ -335,13 +336,13 @@
             dq_out[g] = (dq * scale).T.astype(jnp.bfloat16)
 
     def step(i, carry):
+        @pl.when((i >= LAG_TOTAL) & (i < nh + LAG_TOTAL))
+        def _():
+            totals(i - LAG_TOTAL)
+
         @pl.when(i + AHEAD < nh)
         def _():
             send_head(i + AHEAD)
-
-        @pl.when((i >= LAG_TOTAL) & (i < nh + LAG_TOTAL))
-        def _():
-            totals(i - LAG_TOTAL)
 
         @pl.when((i >= LAG_GRAD) & (i < nh + LAG_GRAD))
         def _():

time: 54.5 us -> 54.2 us (level)
  no operation moved by 1% of the time
where the time goes in v3:
time: 54.2 us; the launch traced here: 53.8 us
  Pallas kernels  53.1 us (98%)
  between operations  0.64 us (1%)
    pallas_call x1, Pallas kernels, per_device(): pl.pallas_call(functools.partial(kernel, seq_size, heads, 1.0 / math.sqrt...  51.8 us
    pallas_call x1, Pallas kernels, per_device(): pl.pallas_call(store, out_shape=(out, out, out), in_specs=[vmem_spec] * 3...  1.3 us

profile of v3, /device:TPU:1, one launch (start us, length us, event | category | flops | bytes accessed | tf_op | source)
XLA Modules:
  0.0 53.8 jit_solution(11827362728005571569)
XLA Ops:
  0.6 51.8 %block_attention.1 = (bf16[20,128,128]{2,1,0:T(8,128)(2,1)S(1)}, bf16[20,128,128]{2,1,0:T(8,128)(2,1)S(1)}, bf16[20,128,128]{2,1,0:T(8,128)(2,1)S(1)}) custom-call(bf16[20,128,128]{2,1,0:T(8,128)(2,1)} %bitcast.8, bf16[20,128,128]{2,1,0:T(8,128)(2,1)} %bitcast.9, bf16[20,128,128]{2,1,0:T(8,128)(2,1)} %bitcast.10, bf16[20,128,128]{2,1,0:T(8,128)(2,1)} %bitcast.11, ...), custom_call_target="tpu_custom_call" | custom-call | tf_op jit(solution)/shard_map/block_attention/pallas_call | solution.py:407
  52.5 1.3 %store_gradients.1 = (bf16[20,128,128]{2,1,0:T(8,128)(2,1)}, bf16[20,128,128]{2,1,0:T(8,128)(2,1)}, bf16[20,128,128]{2,1,0:T(8,128)(2,1)}) custom-call(bf16[20,128,128]{2,1,0:T(8,128)(2,1)S(1)} %get-tuple-element.9.dq_ref, bf16[20,128,128]{2,1,0:T(8,128)(2,1)S(1)} %get-tuple-element.10.dk_ref, bf16[20,128,128]{2,1,0:T(8,128)(2,1)S(1)} %get-tuple-element.11.dv_ref), custom_call_target="tpu_custom_call" | custom-call | tf_op jit(solution)/shard_map/store_gradients/pallas_call | solution.py:453
